TPU v7x, 32 devices: a whole 2x2x4 slice. The times are simulated.
32 devices in a mesh: dp: 16 (over z, y, core), seq: 2 (over x).
Axes of the slice: x: 2, y: 2, z: 4, core: 2. Of those that a mesh axis runs over, the one named last changes fastest.
Arguments:
- clip_tokens: bfloat16 [16, 1024, 1024], P('dp', 'seq'), may hold values from -6 to 6
- adapter_index: int32 [16], P('dp'), may hold values from 0 to 7
- ln1_gain: float32 [1024], replicated, may hold values from 0.25 to 1.75
- ln1_bias: float32 [1024], replicated, may hold values from -1.8 to 1.8
- qkv_weight: bfloat16 [1024, 3072], replicated, may hold values from -0.1875 to 0.1875
- qkv_bias: float32 [3072], replicated, may hold values from -1.8 to 1.8
- qkv_down: bfloat16 [8, 16, 1024], replicated, may hold values from -0.1875 to 0.1875
- qkv_up: bfloat16 [8, 16, 3072], replicated, may hold values from -1.5 to 1.5
- out_weight: bfloat16 [1024, 1024], replicated, may hold values from -3 to 3
- out_bias: float32 [1024], replicated, may hold values from -1.8 to 1.8
- out_down: bfloat16 [8, 16, 1024], replicated, may hold values from -3 to 3
- out_up: bfloat16 [8, 16, 1024], replicated, may hold values from -1.5 to 1.5
- ln2_gain: float32 [1024], replicated, may hold values from 0.25 to 1.75
- ln2_bias: float32 [1024], replicated, may hold values from -1.8 to 1.8
- fc1_weight: bfloat16 [1024, 4096], replicated, may hold values from -0.1875 to 0.1875
- fc1_bias: float32 [4096], replicated, may hold values from -1.8 to 1.8
- fc1_down: bfloat16 [8, 16, 1024], replicated, may hold values from -0.1875 to 0.1875
- fc1_up: bfloat16 [8, 16, 4096], replicated, may hold values from -1.5 to 1.5
- fc2_weight: bfloat16 [4096, 1024], replicated, may hold values from -0.09375 to 0.09375
- fc2_bias: float32 [1024], replicated, may hold values from -1.8 to 1.8
- fc2_down: bfloat16 [8, 16, 4096], replicated, may hold values from -0.09375 to 0.09375
- fc2_up: bfloat16 [8, 16, 1024], replicated, may hold values from -1.5 to 1.5
- cotangent: bfloat16 [16, 1024, 1024], P('dp', 'seq'), may hold values from -6 to 6
Outputs:
- block_output: bfloat16 [16, 1024, 1024], P('dp', 'seq')
- input_grad: float32 [16, 1024, 1024], P('dp', 'seq')
- grad_qkv_down: float32 [8, 16, 1024], replicated
- grad_qkv_up: float32 [8, 16, 3072], replicated
- grad_out_down: float32 [8, 16, 1024], replicated
- grad_out_up: float32 [8, 16, 1024], replicated
- grad_fc1_down: float32 [8, 16, 1024], replicated
- grad_fc1_up: float32 [8, 16, 4096], replicated
- grad_fc2_down: float32 [8, 16, 4096], replicated
- grad_fc2_up: float32 [8, 16, 1024], replicated
All inputs are finite; a program needn't handle non-finite values.
Results may differ from a plain program's by a relative error of at most 0.023.
Values may be sent and summed in bfloat16 or wider, within the bound.
No kernel may reach another device: no remote copies, remote signals or barrier semaphores. Data moves between devices by JAX's collectives and lax.ppermute only.
A program may use at most 192 MiB of HBM per device.

v0:
```python
import jax
import jax.numpy as jnp
from jax import lax
from jax.sharding import PartitionSpec as P

HEADS = 16
HD = 64
FF = 4096
NADAPT = 8
GRID = 16
EPSILON = 1e-06
span_keys = 512


def norm_rows(values, gain, shift):
    centre = values - jnp.mean(values, axis=-1, keepdims=True)
    spread = lax.rsqrt(jnp.mean(centre * centre, axis=-1, keepdims=True) + EPSILON)
    normed = centre * spread
    return (normed * gain + shift, normed, spread)


def norm_back(grad_rows, normed, spread, gain):
    scaled = grad_rows * gain
    first_mean = jnp.mean(scaled, axis=-1, keepdims=True)
    second_mean = jnp.mean(scaled * normed, axis=-1, keepdims=True)
    return spread * (scaled - first_mean - normed * second_mean)


def rotary_tables(first_token, count_rows, head_size, grid_side):
    half_size = head_size // 2
    side_pairs = half_size // 3
    lead_pairs = half_size - 2 * side_pairs
    token_index = first_token + jnp.arange(count_rows, dtype=jnp.int32)
    frame = token_index // (grid_side * grid_side)
    row_pos = token_index // grid_side % grid_side
    col_pos = token_index % grid_side
    pair_index = jnp.arange(half_size, dtype=jnp.int32)
    axis_pick = jnp.where(
        pair_index < lead_pairs, 0, jnp.where(pair_index < lead_pairs + side_pairs, 1, 2)
    )
    local_pair = jnp.where(
        axis_pick == 0,
        pair_index,
        jnp.where(axis_pick == 1, pair_index - lead_pairs, pair_index - lead_pairs - side_pairs),
    )
    total_pairs = jnp.where(axis_pick == 0, lead_pairs, side_pairs)
    frequency = jnp.power(
        10000.0, -local_pair.astype(jnp.float32) / total_pairs.astype(jnp.float32)
    )
    position = jnp.where(
        axis_pick[None, :] == 0,
        frame[:, None],
        jnp.where(axis_pick[None, :] == 1, row_pos[:, None], col_pos[:, None]),
    ).astype(jnp.float32)
    angles = position * frequency[None, :]
    return (jnp.cos(angles), jnp.sin(angles))


def rotate(values, cosine, sine):
    half_size = values.shape[-1] // 2
    first_half = values[..., :half_size]
    second_half = values[..., half_size:]
    cos_rows = cosine[:, None, :]
    sin_rows = sine[:, None, :]
    return jnp.concatenate(
        [
            first_half * cos_rows - second_half * sin_rows,
            first_half * sin_rows + second_half * cos_rows,
        ],
        axis=-1,
    )


def unrotate(values, cosine, sine):
    half_size = values.shape[-1] // 2
    first_half = values[..., :half_size]
    second_half = values[..., half_size:]
    cos_rows = cosine[:, None, :]
    sin_rows = sine[:, None, :]
    return jnp.concatenate(
        [
            first_half * cos_rows + second_half * sin_rows,
            second_half * cos_rows - first_half * sin_rows,
        ],
        axis=-1,
    )


def project(inputs, weight, bias_row, down_pick, up_pick):
    low_rank = jnp.einsum(
        "crd,cad->cra", inputs, down_pick, preferred_element_type=jnp.float32
    ).astype(jnp.bfloat16)
    main_part = jnp.einsum("crd,de->cre", inputs, weight, preferred_element_type=jnp.float32)
    side_part = jnp.einsum("cra,cae->cre", low_rank, up_pick, preferred_element_type=jnp.float32)
    return (main_part + bias_row + side_part, low_rank)


def project_back(grad_low, inputs, low_rank, weight, down_pick, up_pick):
    main_part = jnp.einsum("cre,de->crd", grad_low, weight, preferred_element_type=jnp.float32)
    rank_grad = jnp.einsum(
        "cre,cae->cra", grad_low, up_pick, preferred_element_type=jnp.float32
    ).astype(jnp.bfloat16)
    backward = main_part + jnp.einsum(
        "cra,cad->crd", rank_grad, down_pick, preferred_element_type=jnp.float32
    )
    grad_up = jnp.einsum("cra,cre->cae", low_rank, grad_low, preferred_element_type=jnp.float32)
    grad_down = jnp.einsum("cra,crd->cad", rank_grad, inputs, preferred_element_type=jnp.float32)
    return (backward, grad_down, grad_up)


def over_blocks(block_step, carried, key_rows, value_rows, first_row):
    key_count = key_rows.shape[1]
    block_size = min(key_count, span_keys)
    full_blocks = key_count // block_size

    def one_block(number, inner):
        offset = number * block_size
        return block_step(
            inner,
            lax.dynamic_slice_in_dim(key_rows, offset, block_size, 1),
            lax.dynamic_slice_in_dim(value_rows, offset, block_size, 1),
            first_row + offset,
        )

    carried = lax.fori_loop(0, full_blocks, one_block, carried)
    return carried


def body(
    clip_tokens,
    adapter_index,
    ln1_gain,
    ln1_bias,
    qkv_weight,
    qkv_bias,
    qkv_down,
    qkv_up,
    out_weight,
    out_bias,
    out_down,
    out_up,
    ln2_gain,
    ln2_bias,
    fc1_weight,
    fc1_bias,
    fc1_down,
    fc1_up,
    fc2_weight,
    fc2_bias,
    fc2_down,
    fc2_up,
    cotangent,
):
    clip_count, row_count, model_width = clip_tokens.shape
    score_scale = HD ** (-0.5)
    head_shape = (clip_count, row_count, HEADS, HD)
    onehot = (adapter_index[:, None] == jnp.arange(NADAPT, dtype=jnp.int32)[None, :]).astype(
        jnp.bfloat16
    )

    def select(table_rows):
        return jnp.einsum(
            "ca,ard->crd", onehot, table_rows, preferred_element_type=jnp.float32
        ).astype(jnp.bfloat16)

    picks = [
        select(table_rows)
        for table_rows in (qkv_down, qkv_up, out_down, out_up, fc1_down, fc1_up, fc2_down, fc2_up)
    ]
    inputs = clip_tokens.astype(jnp.float32)
    first_norm, first_normed, first_spread = norm_rows(inputs, ln1_gain, ln1_bias)
    first_in = first_norm.astype(jnp.bfloat16)
    qkv_pre, rank_qkv = project(first_in, qkv_weight, qkv_bias, picks[0], picks[1])
    cosine, sine = rotary_tables(lax.axis_index("seq") * row_count, row_count, HD, GRID)
    query_heads = rotate(qkv_pre[..., :model_width].reshape(head_shape), cosine, sine).astype(
        jnp.bfloat16
    )
    key_low = (
        rotate(qkv_pre[..., model_width : 2 * model_width].reshape(head_shape), cosine, sine)
        .astype(jnp.bfloat16)
        .reshape(clip_count, row_count, model_width)
    )
    value_low = qkv_pre[..., 2 * model_width :].astype(jnp.bfloat16)

    def forward_step(carried, key_rows, value_rows, offset):
        row_max, row_sum, weighted = carried
        key_heads = key_rows.reshape(clip_count, key_rows.shape[1], HEADS, HD)
        value_heads = value_rows.reshape(clip_count, value_rows.shape[1], HEADS, HD)
        scores = (
            jnp.einsum(
                "cqhd,ckhd->chqk", query_heads, key_heads, preferred_element_type=jnp.float32
            )
            * score_scale
        )
        new_max = jnp.maximum(row_max, jnp.max(scores, axis=-1))
        weights = jnp.exp(scores - new_max[..., None])
        factor = jnp.exp(row_max - new_max)
        row_sum = row_sum * factor + jnp.sum(weights, axis=-1)
        update = jnp.einsum(
            "chqk,ckhd->cqhd",
            weights.astype(jnp.bfloat16),
            value_heads,
            preferred_element_type=jnp.float32,
        )
        weighted = weighted * jnp.transpose(factor, (0, 2, 1))[..., None] + update
        return (new_max, row_sum, weighted)

    init_state = (
        jnp.full((clip_count, HEADS, row_count), -1e30, jnp.float32),
        jnp.zeros((clip_count, HEADS, row_count), jnp.float32),
        jnp.zeros(head_shape, jnp.float32),
    )
    key_all, value_all = (
        lax.all_gather(key_low, "seq", axis=1, tiled=True),
        lax.all_gather(value_low, "seq", axis=1, tiled=True),
    )
    row_max, row_sum, weighted = over_blocks(forward_step, init_state, key_all, value_all, 0)
    out_heads = weighted / jnp.transpose(row_sum, (0, 2, 1))[..., None]
    log_total = row_max + jnp.log(row_sum)
    mixed_low = out_heads.reshape(clip_count, row_count, model_width).astype(jnp.bfloat16)
    attn_pre, rank_out = project(mixed_low, out_weight, out_bias, picks[2], picks[3])
    middle = inputs + attn_pre
    second_norm, second_normed, second_spread = norm_rows(middle, ln2_gain, ln2_bias)
    second_in = second_norm.astype(jnp.bfloat16)
    hidden, rank_fc1 = project(second_in, fc1_weight, fc1_bias, picks[4], picks[5])

    def exact_gelu(values):
        return jax.nn.gelu(values, approximate=False)

    active, gelu_back = jax.vjp(exact_gelu, hidden)
    active_low = active.astype(jnp.bfloat16)
    fc2_pre, rank_fc2 = project(active_low, fc2_weight, fc2_bias, picks[6], picks[7])
    block_output = (middle + fc2_pre).astype(jnp.bfloat16)
    grad_active, down_fc2, up_fc2 = project_back(
        cotangent, active_low, rank_fc2, fc2_weight, picks[6], picks[7]
    )
    grad_hidden = gelu_back(grad_active)[0].astype(jnp.bfloat16)
    grad_second, down_fc1, up_fc1 = project_back(
        grad_hidden, second_in, rank_fc1, fc1_weight, picks[4], picks[5]
    )
    grad_middle = cotangent.astype(jnp.float32) + norm_back(
        grad_second, second_normed, second_spread, ln2_gain
    )
    grad_mixed, down_out, up_out = project_back(
        grad_middle.astype(jnp.bfloat16), mixed_low, rank_out, out_weight, picks[2], picks[3]
    )
    grad_heads = grad_mixed.astype(jnp.bfloat16).reshape(head_shape)
    row_delta = jnp.transpose(
        jnp.sum(grad_heads.astype(jnp.float32) * out_heads, axis=-1), (0, 2, 1)
    )

    def score_block(query_rows, grad_rows, log_rows, delta_rows, key_heads, value_heads):
        scores = (
            jnp.einsum("cqhd,ckhd->chqk", query_rows, key_heads, preferred_element_type=jnp.float32)
            * score_scale
        )
        attn_prob = jnp.exp(scores - log_rows[..., None])
        grad_prob = jnp.einsum(
            "cqhd,ckhd->chqk", grad_rows, value_heads, preferred_element_type=jnp.float32
        )
        grad_score = (attn_prob * (grad_prob - delta_rows[..., None])).astype(jnp.bfloat16)
        return (attn_prob, grad_score)

    def backward_step(carried, key_rows, value_rows, offset):
        grad_query, key_full, value_full = carried
        key_heads = key_rows.reshape(clip_count, key_rows.shape[1], HEADS, HD)
        value_heads = value_rows.reshape(clip_count, value_rows.shape[1], HEADS, HD)
        attn_prob, grad_score = score_block(
            query_heads, grad_heads, log_total, row_delta, key_heads, value_heads
        )
        grad_query = (
            grad_query
            + jnp.einsum(
                "chqk,ckhd->cqhd", grad_score, key_heads, preferred_element_type=jnp.float32
            )
            * score_scale
        )
        key_part = (
            jnp.einsum(
                "chqk,cqhd->ckhd", grad_score, query_heads, preferred_element_type=jnp.float32
            )
            * score_scale
        )
        value_part = jnp.einsum(
            "chqk,cqhd->ckhd",
            attn_prob.astype(jnp.bfloat16),
            grad_heads,
            preferred_element_type=jnp.float32,
        )
        key_full = lax.dynamic_update_slice_in_dim(
            key_full, key_part.reshape(clip_count, key_rows.shape[1], model_width), offset, 1
        )
        value_full = lax.dynamic_update_slice_in_dim(
            value_full, value_part.reshape(clip_count, key_rows.shape[1], model_width), offset, 1
        )
        return (grad_query, key_full, value_full)

    whole_rows = row_count * lax.axis_size("seq")
    back_init = (
        jnp.zeros(head_shape, jnp.float32),
        jnp.zeros((clip_count, whole_rows, model_width), jnp.float32),
        jnp.zeros((clip_count, whole_rows, model_width), jnp.float32),
    )
    back_result = over_blocks(backward_step, back_init, key_all, value_all, 0)
    grad_query, key_full, value_full = back_result
    key_grad, value_grad = (
        lax.psum_scatter(
            key_full.astype(jnp.bfloat16), "seq", scatter_dimension=1, tiled=True
        ).astype(jnp.float32),
        lax.psum_scatter(
            value_full.astype(jnp.bfloat16), "seq", scatter_dimension=1, tiled=True
        ).astype(jnp.float32),
    )
    grad_qkv = jnp.concatenate(
        [
            unrotate(grad_query, cosine, sine).reshape(clip_count, row_count, model_width),
            unrotate(key_grad.reshape(head_shape), cosine, sine).reshape(
                clip_count, row_count, model_width
            ),
            value_grad,
        ],
        axis=-1,
    ).astype(jnp.bfloat16)
    grad_first, down_qkv, up_qkv = project_back(
        grad_qkv, first_in, rank_qkv, qkv_weight, picks[0], picks[1]
    )
    input_grad = grad_middle + norm_back(grad_first, first_normed, first_spread, ln1_gain)
    packed_clip = jnp.concatenate(
        [down_qkv, up_qkv, down_out, up_out, down_fc1, up_fc1, down_fc2, up_fc2], axis=2
    )
    packed = jnp.einsum(
        "ca,crw->arw", onehot.astype(jnp.float32), packed_clip, precision=lax.Precision.HIGHEST
    )
    summed = lax.psum(packed.astype(jnp.bfloat16), "dp")
    owned = lax.psum_scatter(summed, "seq", scatter_dimension=2, tiled=True).astype(jnp.float32)
    gathered = lax.all_gather(owned.astype(jnp.bfloat16), "seq", axis=2, tiled=True).astype(
        owned.dtype
    )
    widths = [
        model_width,
        3 * model_width,
        model_width,
        model_width,
        model_width,
        FF,
        FF,
        model_width,
    ]
    results = []
    position = 0
    for span_width in widths:
        results.append(gathered[:, :, position : position + span_width])
        position = position + span_width
    return (
        block_output,
        input_grad,
        results[0],
        results[1],
        results[2],
        results[3],
        results[4],
        results[5],
        results[6],
        results[7],
    )


def solution(mesh):
    return jax.shard_map(
        body,
        mesh=mesh,
        in_specs=(
            P("dp", "seq", None),
            P("dp"),
            P(),
            P(),
            P(),
            P(),
            P(),
            P(),
            P(),
            P(),
            P(),
            P(),
            P(),
            P(),
            P(),
            P(),
            P(),
            P(),
            P(),
            P(),
            P(),
            P(),
            P("dp", "seq", None),
        ),
        out_specs=(
            P("dp", "seq", None),
            P("dp", "seq", None),
            P(),
            P(),
            P(),
            P(),
            P(),
            P(),
            P(),
            P(),
        ),
        check_vma=False,
    )
```

profile of v0, /device:TPU:0, one launch (start us, length us, event | category | flops | bytes accessed | tf_op | source)
XLA Modules:
  0.0 613.7 jit_solution(2214221213722635700)
XLA Ops:
  7.2 1.6 convert_reduce_fusion
  8.8 1.6 fusion.44
  12.4 6.8 %fusion.113 = f32[512,3072]{1,0:T(8,128)S(1)} fusion(bf16[1024,3072]{1,0:T(8,128)(2,1)} %param.31, bf16[1,512,1024]{2,1,0:T(8,128)(2,1)} %param.27, f32[1024]{0:T(1024)} %param.30, f32[1024]{0:T(1024)} %param.29, f32[512]{0:T(512)S(1)} %add_rsqrt_fusion.1, f32[512]{0:T(512)S(1)} %broadcast_multiply_fusion.5), kind=kOutput, calls=%fused_computation.224 | convolution fusion | flops 3224371200 | bytes 13643776 | tf_op jit(solution)/shard_map/crd,de->cre/dot_general | solution.py:93
  21.6 2.6 copy-done.13
  25.5 4.8 fusion.116
  30.3 2.9 copy.44
  33.2 3.0 copy.43
  36.6 4.2 subtract_convert_fusion.2
  42.9 1.8 fusion.75
  46.9 1.8 fusion.73
  50.1 2.5 fusion.66
  52.7 3.2 fusion.64
  55.9 10.4 %fusion.62 = f32[512,4096]{1,0:T(8,128)} fusion(bf16[4096,1024]{1,0:T(8,128)(2,1)} %param.45, bf16[1,512,1024]{2,1,0:T(8,128)(2,1)S(1)} %copy-done.23), kind=kOutput, calls=%fused_computation.125 | convolution fusion | flops 4294967296 | bytes 17825792 | tf_op jit(solution)/shard_map/cre,de->crd/dot_general | solution.py:99
  66.3 3.9 copy.45
  70.2 26.5 %all-gather.4.cloned.1.call-done = bf16[1,1024,1024]{1,2,0:T(8,128)(2,1)} async-done(((bf16[1,512,1024]{1,2,0:T(8,128)(2,1)}), bf16[1,1024,1024]{1,2,0:T(8,128)(2,1)}) %all-gather.4.cloned.1.call-update) | async-done | bytes 2097168 | tf_op jit(solution)/shard_map/all_gather | solution.py:214
  96.6 60.7 %while.36 = (s32[]{:T(128)}, f32[1,16,512]{2,1,0:T(8,128)S(1)}, f32[1,16,512]{2,1,0:T(8,128)S(1)}, f32[1,512,16,64]{1,3,2,0:T(8,128)}, bf16[1,1024,1024]{1,2,0:T...) while((s32[]{:T(128)}, f32[1,16,512]{2,1,0:T(8,128)S(1)}, ...), condition=%wide.region_5.6_spmd.clone, body=%wide.region_2.5_spmd.clone.sunk | while | flops 1108918272 | bytes 66584780 | solution.py:125
  96.6 2.6 constant_dynamic-slice_fusion.7
  99.3 8.2 %bitcast_reduce_fusion.2 = (f32[16,512]{1,0:T(8,128)S(1)}, f32[16,512,512]{2,1,0:T(8,128)}) fusion(bf16[512,16,64]{0,2,1:T(8,128)(2,1)S(1)} %bitcast.339, bf16[1,512,16,64]{1,3,2,0:T(8,128)(2,1)S(1)} %get-tuple-element.629), kind=kOutput, calls=%fused_computation.1.clone.1 | convolution fusion | flops 545251328 | bytes 18907136 | tf_op jit(solution)/shard_map/while/body/eval_jaxpr/cqhd,ckhd->chqk/dot_general | solution.py:190
  107.5 8.7 %fusion.188 = f32[16,512]{1,0:T(8,128)S(1)} fusion(f32[16,512,512]{2,1,0:T(8,128)} %get-tuple-element.587, f32[16,512]{1,0:T(8,128)S(1)} %bitcast.342), kind=kLoop, calls=%fused_computation.4.clone.1 | loop fusion | flops 12574720 | bytes 16842752 | tf_op jit(solution)/shard_map/while/body/eval_jaxpr/reduce_sum | solution.py:198
  116.2 10.3 %bitcast_add_fusion.8 = f32[1,512,16,64]{1,3,2,0:T(8,128)} fusion(f32[1,512,16,64]{1,3,2,0:T(8,128)} %get-tuple-element.616, bf16[512,16,64]{0,2,1:T(8,128)(2,1)S(1)} %bitcast.337, f32[16,512,512]{2,1,0:T(8,128)} %get-tuple-element.587, f32[16,512]{1,0:T(8,128)S(1)} %bitcast.343, f32[512,16]{0,1:T(8,128)S(1)} %get-tuple-element.589, pred[]{:T(512)S(6)} %compare.27), kind=kOutput, calls=%fused_computation.8.clone.1 | convolution fusion | flops 551026688 | bytes 22085632 | tf_op jit(solution)/shard_map/while/body/eval_jaxpr/chqk,ckhd->cqhd/dot_general | solution.py:199
  126.5 2.6 constant_dynamic-slice_fusion.7
  129.1 8.2 %bitcast_reduce_fusion.2 = (f32[16,512]{1,0:T(8,128)S(1)}, f32[16,512,512]{2,1,0:T(8,128)}) fusion(bf16[512,16,64]{0,2,1:T(8,128)(2,1)S(1)} %bitcast.339, bf16[1,512,16,64]{1,3,2,0:T(8,128)(2,1)S(1)} %get-tuple-element.629), kind=kOutput, calls=%fused_computation.1.clone.1 | convolution fusion | flops 545251328 | bytes 18907136 | tf_op jit(solution)/shard_map/while/body/eval_jaxpr/cqhd,ckhd->chqk/dot_general | solution.py:190
  137.4 8.7 %fusion.188 = f32[16,512]{1,0:T(8,128)S(1)} fusion(f32[16,512,512]{2,1,0:T(8,128)} %get-tuple-element.587, f32[16,512]{1,0:T(8,128)S(1)} %bitcast.342), kind=kLoop, calls=%fused_computation.4.clone.1 | loop fusion | flops 12574720 | bytes 16842752 | tf_op jit(solution)/shard_map/while/body/eval_jaxpr/reduce_sum | solution.py:198
  146.1 10.9 %bitcast_add_fusion.8 = f32[1,512,16,64]{1,3,2,0:T(8,128)} fusion(f32[1,512,16,64]{1,3,2,0:T(8,128)} %get-tuple-element.616, bf16[512,16,64]{0,2,1:T(8,128)(2,1)S(1)} %bitcast.337, f32[16,512,512]{2,1,0:T(8,128)} %get-tuple-element.587, f32[16,512]{1,0:T(8,128)S(1)} %bitcast.343, f32[512,16]{0,1:T(8,128)S(1)} %get-tuple-element.589, pred[]{:T(512)S(6)} %compare.27), kind=kOutput, calls=%fused_computation.8.clone.1 | convolution fusion | flops 551026688 | bytes 22085632 | tf_op jit(solution)/shard_map/while/body/eval_jaxpr/chqk,ckhd->cqhd/dot_general | solution.py:199
  157.4 2.0 fusion.68
  163.8 1.7 slice-done.1
  165.5 4.5 fusion.121
  170.0 21.3 %multiply_convert_fusion.2 = (bf16[512,4096]{1,0:T(8,128)(2,1)}, f32[512,4096]{1,0:T(8,128)}, f32[512,4096]{1,0:T(8,128)}) fusion(bf16[512,16]{0,1:T(8,128)(2,1)S(1)} %convolution_convert_fusion.4, bf16[1,16,4096]{2,0,1:T(2,128)(2,1)S(1)} %fusion.66, f32[512,4096]{1,0:T(8,128)S(1)} %fusion.121, f32[4096]{0:T(1024)S(1)} %copy-done.76), kind=kOutput, calls=%fused_computation.42 | convolution fusion | flops 207618048 | bytes 29523968 | tf_op jit(solution)/shard_map/cra,cae->cre/dot_general | solution.py:94
  191.4 10.5 %add_convert_fusion = bf16[512,4096]{1,0:T(8,128)(2,1)S(1)} fusion(f32[512,4096]{1,0:T(8,128)} %get-tuple-element.441, f32[512,4096]{1,0:T(8,128)} %fusion.62, f32[512,4096]{1,0:T(8,128)} %get-tuple-element.473, bf16[16,512]{1,0:T(8,128)(2,1)S(1)} %copy-done.57, bf16[1,16,4096]{2,0,1:T(2,128)(2,1)S(1)} %copy-done.38), kind=kOutput, calls=%fused_computation.41 | convolution fusion | flops 98566144 | bytes 29507584 | tf_op jit(solution)/shard_map/cra,cad->crd/dot_general | solution.py:103
  201.9 4.5 fusion.123
  207.6 2.0 fusion.45
  209.6 1.8 reduce_sum.100
  211.4 3.2 fusion.47
  218.0 2.0 multiply_reduce_fusion
  220.0 1.6 broadcast.568
  221.6 1.6 broadcast.568.clone
  223.2 85.0 %while.37 = (s32[]{:T(128)}, f32[1,512,16,64]{1,3,2,0:T(8,128)}, bf16[1,1024,1024]{1,2,0:T(8,128)(2,1)}, bf16[1,1024,1024]{1,2,0:T(8,128)(2,1)}, bf16[1,1024,102...) while((s32[]{:T(128)}, f32[1,512,16,64]{1,3,2,0:T(8,128)}, ...), condition=%wide.region_12.13_spmd.clone, body=%wide.region_11.12_spmd.clone.sunk | while | flops 2720530432 | bytes 139559264 | solution.py:125
  224.7 8.2 %fusion.199 = f32[16,512,512]{2,1,0:T(8,128)} fusion(bf16[512,16,64]{0,2,1:T(8,128)(2,1)S(1)} %bitcast.333, bf16[1,512,16,64]{1,3,2,0:T(8,128)(2,1)S(1)} %get-tuple-element.668), kind=kOutput, calls=%fused_computation.33.clone.1 | convolution fusion | flops 536870912 | bytes 18874368 | tf_op jit(solution)/shard_map/while/body/eval_jaxpr/cqhd,ckhd->chqk/dot_general | solution.py:254
  233.0 10.2 %multiply_convert_fusion.4 = bf16[16,512,512]{2,1,0:T(8,128)(2,1)} fusion(f32[16,512,512]{2,1,0:T(8,128)} %fusion.199, bf16[512,16,64]{0,2,1:T(8,128)(2,1)S(1)} %bitcast.340, f32[16,512]{1,0:T(8,128)S(1)} %bitcast.355, f32[16,512]{1,0:T(8,128)S(1)} %bitcast.350, bf16[1,512,16,64]{1,3,2,0:T(8,128)(2,1)S(1)} %get-tuple-element.671), kind=kOutput, calls=%fused_computation.20.clone.1 | convolution fusion | flops 557842432 | bytes 27328512 | tf_op jit(solution)/shard_map/while/body/eval_jaxpr/cqhd,ckhd->chqk/dot_general | solution.py:258
  243.3 6.2 %bitcast_add_fusion.9 = f32[1,512,16,64]{1,3,2,0:T(8,128)} fusion(f32[1,512,16,64]{1,3,2,0:T(8,128)} %get-tuple-element.650, bf16[512,16,64]{0,2,1:T(8,128)(2,1)S(1)} %bitcast.334, bf16[16,512,512]{2,1,0:T(8,128)(2,1)} %multiply_convert_fusion.4, pred[]{:T(512)S(6)} %compare.28), kind=kOutput, calls=%fused_computation.28.clone.1 | convolution fusion | flops 538443776 | bytes 13631489 | tf_op jit(solution)/shard_map/while/body/eval_jaxpr/chqk,ckhd->cqhd/dot_general | solution.py:273
  249.4 7.5 %fusion.200 = bf16[16,512,64]{1,2,0:T(8,128)(2,1)S(1)} fusion(f32[16,512,512]{2,1,0:T(8,128)} %fusion.199, f32[16,512]{1,0:T(8,128)S(1)} %bitcast.351, bf16[1,512,16,64]{1,3,2,0:T(8,128)(2,1)S(1)} %get-tuple-element.671), kind=kOutput, calls=%fused_computation.23.clone.1 | convolution fusion | flops 549453824 | bytes 18907136 | tf_op jit(solution)/shard_map/while/body/eval_jaxpr/chqk,cqhd->ckhd/dot_general | solution.py:284
  257.0 6.2 %convolution_multiply_fusion.2 = bf16[16,512,64]{1,2,0:T(8,128)(2,1)S(1)} fusion(bf16[16,512,512]{2,1,0:T(8,128)(2,1)} %multiply_convert_fusion.4, bf16[1,512,16,64]{1,3,2,0:T(8,128)(2,1)S(1)} %get-tuple-element.668), kind=kOutput, calls=%fused_computation.29.clone.1 | convolution fusion | flops 537919488 | bytes 10485760 | tf_op jit(solution)/shard_map/while/body/eval_jaxpr/chqk,cqhd->ckhd/dot_general | solution.py:279
  266.8 8.2 %fusion.199 = f32[16,512,512]{2,1,0:T(8,128)} fusion(bf16[512,16,64]{0,2,1:T(8,128)(2,1)S(1)} %bitcast.333, bf16[1,512,16,64]{1,3,2,0:T(8,128)(2,1)S(1)} %get-tuple-element.668), kind=kOutput, calls=%fused_computation.33.clone.1 | convolution fusion | flops 536870912 | bytes 18874368 | tf_op jit(solution)/shard_map/while/body/eval_jaxpr/cqhd,ckhd->chqk/dot_general | solution.py:254
  275.1 10.2 %multiply_convert_fusion.4 = bf16[16,512,512]{2,1,0:T(8,128)(2,1)} fusion(f32[16,512,512]{2,1,0:T(8,128)} %fusion.199, bf16[512,16,64]{0,2,1:T(8,128)(2,1)S(1)} %bitcast.340, f32[16,512]{1,0:T(8,128)S(1)} %bitcast.355, f32[16,512]{1,0:T(8,128)S(1)} %bitcast.350, bf16[1,512,16,64]{1,3,2,0:T(8,128)(2,1)S(1)} %get-tuple-element.671), kind=kOutput, calls=%fused_computation.20.clone.1 | convolution fusion | flops 557842432 | bytes 27328512 | tf_op jit(solution)/shard_map/while/body/eval_jaxpr/cqhd,ckhd->chqk/dot_general | solution.py:258
  285.4 6.8 %bitcast_add_fusion.9 = f32[1,512,16,64]{1,3,2,0:T(8,128)} fusion(f32[1,512,16,64]{1,3,2,0:T(8,128)} %get-tuple-element.650, bf16[512,16,64]{0,2,1:T(8,128)(2,1)S(1)} %bitcast.334, bf16[16,512,512]{2,1,0:T(8,128)(2,1)} %multiply_convert_fusion.4, pred[]{:T(512)S(6)} %compare.28), kind=kOutput, calls=%fused_computation.28.clone.1 | convolution fusion | flops 538443776 | bytes 13631489 | tf_op jit(solution)/shard_map/while/body/eval_jaxpr/chqk,ckhd->cqhd/dot_general | solution.py:273
  292.1 7.5 %fusion.200 = bf16[16,512,64]{1,2,0:T(8,128)(2,1)S(1)} fusion(f32[16,512,512]{2,1,0:T(8,128)} %fusion.199, f32[16,512]{1,0:T(8,128)S(1)} %bitcast.351, bf16[1,512,16,64]{1,3,2,0:T(8,128)(2,1)S(1)} %get-tuple-element.671), kind=kOutput, calls=%fused_computation.23.clone.1 | convolution fusion | flops 549453824 | bytes 18907136 | tf_op jit(solution)/shard_map/while/body/eval_jaxpr/chqk,cqhd->ckhd/dot_general | solution.py:284
  299.7 6.2 %convolution_multiply_fusion.2 = bf16[16,512,64]{1,2,0:T(8,128)(2,1)S(1)} fusion(bf16[16,512,512]{2,1,0:T(8,128)(2,1)} %multiply_convert_fusion.4, bf16[1,512,16,64]{1,3,2,0:T(8,128)(2,1)S(1)} %get-tuple-element.668), kind=kOutput, calls=%fused_computation.29.clone.1 | convolution fusion | flops 537919488 | bytes 10485760 | tf_op jit(solution)/shard_map/while/body/eval_jaxpr/chqk,cqhd->ckhd/dot_general | solution.py:279
  309.2 3.5 convolution_convert_fusion.7
  312.7 27.5 %reduce-scatter.4.cloned.1.call-done = bf16[1,512,1024]{1,2,0:T(8,128)(2,1)} async-done(((bf16[1,1024,1024]{1,2,0:T(8,128)(2,1)}), bf16[1,512,1024]{1,2,0:T(8,128)(2,1)}) %reduce-scatter.4.cloned.1.call-update) | async-done | bytes 1048592 | tf_op jit(solution)/shard_map/reduce_scatter | solution.py:307
  340.2 1.5 convert.54
  342.7 31.6 %reduce-scatter.6.cloned.1.call-done = bf16[1,512,1024]{1,2,0:T(8,128)(2,1)} async-done(((bf16[1,1024,1024]{1,2,0:T(8,128)(2,1)}), bf16[1,512,1024]{1,2,0:T(8,128)(2,1)}) %reduce-scatter.6.cloned.1.call-update) | async-done | bytes 1048592 | tf_op jit(solution)/shard_map/reduce_scatter | solution.py:310
  374.3 1.8 convolution_convert_fusion
  376.8 2.6 fusion.32
  383.2 2.6 multiply_convert_fusion.1
  385.9 54.4 %reduce-scatter.8.cloned.1.call-done = bf16[8,16,8192]{2,1,0:T(8,128)(2,1)} async-done(((bf16[8,16,16384]{2,1,0:T(8,128)(2,1)}), bf16[8,16,8192]{2,1,0:T(8,128)(2,1)}) %reduce-scatter.8.cloned.1.call-update) | async-done | bytes 2097168 | tf_op jit(solution)/shard_map/reduce_scatter | solution.py:335
  440.7 101.3 %all-reduce.2.cloned.1.call-done = bf16[8,16,8192]{2,1,0:T(8,128)(2,1)} async-done(((bf16[8,16,8192]{2,1,0:T(8,128)(2,1)}), bf16[8,16,8192]{2,1,0:T(8,128)(2,1)}) %all-reduce.2.cloned.1.call-update) | async-done | bytes 2097168 | tf_op jit(solution)/shard_map/psum | solution.py:334
  542.1 8.3 %fusion.122 = f32[512,1024]{1,0:T(8,128)S(1)} fusion(bf16[512,4096]{1,0:T(8,128)(2,1)} %get-tuple-element.440, bf16[4096,1024]{1,0:T(8,128)(2,1)} %param.45), kind=kOutput, calls=%fused_computation.231 | convolution fusion | flops 4294967296 | bytes 14680064 | tf_op jit(solution)/shard_map/crd,de->cre/dot_general | solution.py:93
  553.0 6.8 %fusion.110 = f32[512,1024]{1,0:T(8,128)S(1)} fusion(bf16[1024,3072]{1,0:T(8,128)(2,1)} %param.31, bf16[512,1024]{0,1:T(8,128)(2,1)S(1)} %bitcast.368, bf16[512,1024]{0,1:T(8,128)(2,1)S(1)} %bitcast.359, bf16[512,1024]{0,1:T(8,128)(2,1)S(1)} %bitcast.362), kind=kOutput, calls=%fused_computation.223 | convolution fusion | flops 3230662656 | bytes 11534336 | tf_op jit(solution)/shard_map/cre,de->crd/dot_general | solution.py:99
  559.8 2.0 fusion.40
  561.8 1.8 reduce_sum.104
  563.6 3.5 fusion.43
  567.2 32.4 %all-gather.8.cloned.1.call-done = bf16[8,16,16384]{2,1,0:T(8,128)(2,1)} async-done(((bf16[8,16,8192]{2,1,0:T(8,128)(2,1)}), bf16[8,16,16384]{2,1,0:T(8,128)(2,1)}) %all-gather.8.cloned.1.call-update) | async-done | bytes 4194320 | tf_op jit(solution)/shard_map/all_gather | solution.py:336
  599.6 3.0 fusion.117
  603.9 2.5 fusion.118
  (252 shorter events, 37.7 us)
Async XLA Ops:
  7.2 153.3 %copy-start = (bf16[1024,1024]{1,0:T(8,128)(2,1)S(1)}, bf16[1024,1024]{1,0:T(8,128)(2,1)}, u32[]{:S(2)}) copy-start(bf16[1024,1024]{1,0:T(8,128)(2,1)} %param.35) | copy-start | bytes 6291460
  7.2 59.1 %all-gather.6.cloned.1.call-start = ((), (), s32[]{:S(2)}) async-start(), calls=%async_computation.4 | async-start | bytes 3145728 | tf_op jit(solution)/shard_map/all_gather | solution.py:215
  8.8 10.5 %copy-start.61 = (f32[512]{0:T(512)}, f32[512]{0:T(512)S(1)}, u32[]{:S(2)}) copy-start(f32[512]{0:T(512)S(1)} %broadcast_multiply_fusion.5) | copy-start | bytes 6148
  10.5 8.8 %copy-start.63 = (f32[512]{0:T(512)}, f32[512]{0:T(512)S(1)}, u32[]{:S(2)}) copy-start(f32[512]{0:T(512)S(1)} %add_rsqrt_fusion.1) | copy-start | bytes 6148
  12.4 6.9 %copy-start.55 = (bf16[1,16,1024]{2,0,1:T(2,128)(2,1)}, bf16[1,16,1024]{2,0,1:T(2,128)(2,1)S(1)}, u32[]{:S(2)}) copy-start(bf16[1,16,1024]{2,0,1:T(2,128)(2,1)S(1)} %fusion.79) | copy-start | bytes 98308
  12.4 6.9 %copy-start.10 = (bf16[1,512,1024]{2,1,0:T(8,128)(2,1)S(1)}, bf16[1,512,1024]{2,1,0:T(8,128)(2,1)}, u32[]{:S(2)}) copy-start(bf16[1,512,1024]{2,1,0:T(8,128)(2,1)} %param.27) | copy-start | bytes 3145732
  12.4 6.9 %copy-start.70 = (f32[1024]{0:T(1024)S(1)}, f32[1024]{0:T(1024)}, u32[]{:S(2)}) copy-start(f32[1024]{0:T(1024)} %param.29) | copy-start | bytes 12292
  12.4 6.9 %copy-start.77 = (f32[1024]{0:T(1024)S(1)}, f32[1024]{0:T(1024)}, u32[]{:S(2)}) copy-start(f32[1024]{0:T(1024)} %param.30) | copy-start | bytes 12292
  12.4 7.5 %copy-start.33 = (bf16[8,16,3072]{2,1,0:T(8,128)(2,1)S(1)}, bf16[8,16,3072]{2,1,0:T(8,128)(2,1)}, u32[]{:S(2)}) copy-start(bf16[8,16,3072]{2,1,0:T(8,128)(2,1)} %param.34) | copy-start | bytes 2359300
  12.4 8.2 %copy-start.68 = (f32[3072]{0:T(1024)S(1)}, f32[3072]{0:T(1024)}, u32[]{:S(2)}) copy-start(f32[3072]{0:T(1024)} %param.32) | copy-start | bytes 36868
  25.4 71.2 %all-gather.4.cloned.1.call-start = ((), (), s32[]{:S(2)}) async-start(), calls=%async_computation.3 | async-start | bytes 3145728 | tf_op jit(solution)/shard_map/all_gather | solution.py:214
  36.6 5.3 copy-start.34
  36.6 5.3 copy-start.36
  36.6 5.3 copy-start.48
  36.6 9.3 %copy-start.22 = (bf16[1,512,1024]{2,1,0:T(8,128)(2,1)S(1)}, bf16[1,512,1024]{2,1,0:T(8,128)(2,1)}, u32[]{:S(2)}) copy-start(bf16[1,512,1024]{2,1,0:T(8,128)(2,1)} %param.49) | copy-start | bytes 3145732
  41.9 298.3 %reduce-scatter.4.cloned.1.call-start = ((), (), s32[]{:S(2)}) async-start(), calls=%async_computation.5 | async-start | bytes 3145728 | tf_op jit(solution)/shard_map/reduce_scatter | solution.py:307
  48.7 7.1 %copy-start.23 = (bf16[1,512,1024]{2,1,0:T(8,128)(2,1)S(1)}, bf16[1,512,1024]{2,1,0:T(8,128)(2,1)}, u32[]{:S(2)}) copy-start(bf16[1,512,1024]{2,1,0:T(8,128)(2,1)} %param.49) | copy-start | bytes 3145732
  107.5 8.7 %copy-start.3 = (bf16[1,512,1024]{1,2,0:T(8,128)(2,1)S(1)}, bf16[1,512,1024]{1,2,0:T(8,128)(2,1)}, u32[]{:S(2)}) copy-start(bf16[1,512,1024]{1,2,0:T(8,128)(2,1)} %get-tuple-element.588) | copy-start | bytes 3145732 | tf_op jit(solution)/shard_map/while
  137.3 8.7 %copy-start.3 = (bf16[1,512,1024]{1,2,0:T(8,128)(2,1)S(1)}, bf16[1,512,1024]{1,2,0:T(8,128)(2,1)}, u32[]{:S(2)}) copy-start(bf16[1,512,1024]{1,2,0:T(8,128)(2,1)} %get-tuple-element.588) | copy-start | bytes 3145732 | tf_op jit(solution)/shard_map/while
  157.3 4.5 copy-start.11
  157.3 4.5 copy-start.42
  157.4 4.5 copy-start.72
  160.5 3.3 slice-start
  161.9 3.6 slice-start.1
  162.6 45.0 %copy-start.5 = (f32[1,512,1024]{2,1,0:T(8,128)}, f32[1,512,1024]{2,1,0:T(8,128)S(1)}, u32[]{:S(2)}) copy-start(f32[1,512,1024]{2,1,0:T(8,128)S(1)} %get-tuple-element.472) | copy-start | bytes 6291460
  163.4 6.6 %copy-start.20 = (bf16[512,1024]{1,0:T(8,128)(2,1)}, bf16[512,1024]{1,0:T(8,128)(2,1)S(1)}, u32[]{:S(2)}) copy-start(bf16[512,1024]{1,0:T(8,128)(2,1)S(1)} %fusion.54) | copy-start | bytes 3145732
  165.5 4.5 copy-start.59
  165.5 4.5 copy-start.76
  170.0 21.3 %copy-start.38 = (bf16[1,16,4096]{2,0,1:T(2,128)(2,1)S(1)}, bf16[1,16,4096]{2,0,1:T(2,128)(2,1)}, u32[]{:S(2)}) copy-start(bf16[1,16,4096]{2,0,1:T(2,128)(2,1)} %fusion.64) | copy-start | bytes 393220
  170.0 21.3 %copy-start.57 = (bf16[16,512]{1,0:T(8,128)(2,1)S(1)}, bf16[16,512]{1,0:T(8,128)(2,1)}, u32[]{:S(2)}) copy-start(bf16[16,512]{1,0:T(8,128)(2,1)} %convolution_convert_fusion.3) | copy-start | bytes 49156
  201.9 4.5 copy-start.17
  207.6 3.8 copy-start.51
  224.7 8.2 %copy-start.4 = (bf16[1,1024,1024]{1,2,0:T(8,128)(2,1)S(1)}, bf16[1,1024,1024]{1,2,0:T(8,128)(2,1)}, u32[]{:S(2)}) copy-start(bf16[1,1024,1024]{1,2,0:T(8,128)(2,1)} %get-tuple-element.670) | copy-start | bytes 6291460 | tf_op jit(solution)/shard_map/while
  256.9 6.2 %copy-start.25 = (bf16[1,1024,1024]{1,2,0:T(8,128)(2,1)S(1)}, bf16[1,1024,1024]{1,2,0:T(8,128)(2,1)}, u32[]{:S(2)}) copy-start(bf16[1,1024,1024]{1,2,0:T(8,128)(2,1)} %get-tuple-element.651) | copy-start | bytes 6291460 | tf_op jit(solution)/shard_map/while
  257.0 6.2 %copy-start.27 = (bf16[1,1024,1024]{1,2,0:T(8,128)(2,1)S(1)}, bf16[1,1024,1024]{1,2,0:T(8,128)(2,1)}, u32[]{:S(2)}) copy-start(bf16[1,1024,1024]{1,2,0:T(8,128)(2,1)} %get-tuple-element.652) | copy-start | bytes 6291460 | tf_op jit(solution)/shard_map/while
  266.8 8.2 %copy-start.4 = (bf16[1,1024,1024]{1,2,0:T(8,128)(2,1)S(1)}, bf16[1,1024,1024]{1,2,0:T(8,128)(2,1)}, u32[]{:S(2)}) copy-start(bf16[1,1024,1024]{1,2,0:T(8,128)(2,1)} %get-tuple-element.670) | copy-start | bytes 6291460 | tf_op jit(solution)/shard_map/while
  299.6 6.2 %copy-start.25 = (bf16[1,1024,1024]{1,2,0:T(8,128)(2,1)S(1)}, bf16[1,1024,1024]{1,2,0:T(8,128)(2,1)}, u32[]{:S(2)}) copy-start(bf16[1,1024,1024]{1,2,0:T(8,128)(2,1)} %get-tuple-element.651) | copy-start | bytes 6291460 | tf_op jit(solution)/shard_map/while
  299.6 6.2 %copy-start.27 = (bf16[1,1024,1024]{1,2,0:T(8,128)(2,1)S(1)}, bf16[1,1024,1024]{1,2,0:T(8,128)(2,1)}, u32[]{:S(2)}) copy-start(bf16[1,1024,1024]{1,2,0:T(8,128)(2,1)} %get-tuple-element.652) | copy-start | bytes 6291460 | tf_op jit(solution)/shard_map/while
  308.2 66.0 %reduce-scatter.6.cloned.1.call-start = ((), (), s32[]{:S(2)}) async-start(), calls=%async_computation.6 | async-start | bytes 3145728 | tf_op jit(solution)/shard_map/reduce_scatter | solution.py:310
  308.8 32.9 %copy-start.2 = (f32[1,512,16,64]{1,3,2,0:T(8,128)S(1)}, f32[1,512,16,64]{1,3,2,0:T(8,128)}, u32[]{:S(2)}) copy-start(f32[1,512,16,64]{1,3,2,0:T(8,128)} %get-tuple-element.310) | copy-start | bytes 6291460
  308.8 32.9 %copy-start.35 = (f32[512,32]{0,1:T(8,128)S(1)}, f32[512,32]{0,1:T(8,128)}, u32[]{:S(2)}) copy-start(f32[512,32]{0,1:T(8,128)} %copy-done.34) | copy-start | bytes 196612
  308.8 32.9 %copy-start.37 = (f32[512,32]{0,1:T(8,128)S(1)}, f32[512,32]{0,1:T(8,128)}, u32[]{:S(2)}) copy-start(f32[512,32]{0,1:T(8,128)} %copy-done.36) | copy-start | bytes 196612
  308.9 131.5 %reduce-scatter.8.cloned.1.call-start = ((), (), s32[]{:S(2)}) async-start(), calls=%async_computation.8 | async-start | bytes 6291456 | tf_op jit(solution)/shard_map/reduce_scatter | solution.py:335
  341.8 32.5 %copy-start.41 = (bf16[1,16,3072]{2,0,1:T(2,128)(2,1)S(1)}, bf16[1,16,3072]{2,0,1:T(2,128)(2,1)}, u32[]{:S(2)}) copy-start(bf16[1,16,3072]{2,0,1:T(2,128)(2,1)} %copy-done.40) | copy-start | bytes 294916
  342.5 33.6 %copy-start.29 = (bf16[1,512,16,64]{1,3,2,0:T(8,128)(2,1)}, bf16[1,512,16,64]{1,3,2,0:T(8,128)(2,1)S(1)}, u32[]{:S(2)}) copy-start(bf16[1,512,16,64]{1,3,2,0:T(8,128)(2,1)S(1)} %pad_maximum_fusion.4) | copy-start | bytes 3145732
  342.6 33.5 %copy-start.31 = (bf16[1,512,16,64]{1,3,2,0:T(8,128)(2,1)}, bf16[1,512,16,64]{1,3,2,0:T(8,128)(2,1)S(1)}, u32[]{:S(2)}) copy-start(bf16[1,512,16,64]{1,3,2,0:T(8,128)(2,1)S(1)} %pad_maximum_fusion.3) | copy-start | bytes 3145732
  342.6 33.5 %copy-start.12 = (bf16[1,512,1024]{2,1,0:T(8,128)(2,1)S(1)}, bf16[1,512,1024]{2,1,0:T(8,128)(2,1)}, u32[]{:S(2)}) copy-start(bf16[1,512,1024]{2,1,0:T(8,128)(2,1)} %param.27) | copy-start | bytes 3145732
  342.6 33.5 %copy-start.62 = (f32[512]{0:T(512)S(1)}, f32[512]{0:T(512)}, u32[]{:S(2)}) copy-start(f32[512]{0:T(512)} %copy-done.61) | copy-start | bytes 6148
  342.6 33.5 %copy-start.64 = (f32[512]{0:T(512)S(1)}, f32[512]{0:T(512)}, u32[]{:S(2)}) copy-start(f32[512]{0:T(512)} %copy-done.63) | copy-start | bytes 6148
  342.7 33.5 %copy-start.71 = (f32[1024]{0:T(1024)S(1)}, f32[1024]{0:T(1024)}, u32[]{:S(2)}) copy-start(f32[1024]{0:T(1024)} %param.29) | copy-start | bytes 12292
  342.7 33.5 %copy-start.78 = (f32[1024]{0:T(1024)S(1)}, f32[1024]{0:T(1024)}, u32[]{:S(2)}) copy-start(f32[1024]{0:T(1024)} %param.30) | copy-start | bytes 12292
  376.2 3.3 copy-start.54
  376.8 3.3 copy-start.21
  376.8 3.3 copy-start.52
  376.8 4.1 copy-start.18
  376.8 4.1 copy-start.60
  385.9 156.1 %all-reduce.2.cloned.1.call-start = ((), (), s32[]{:S(2)}) async-start(), calls=%async_computation.9 | async-start | bytes 4194304 | tf_op jit(solution)/shard_map/psum | solution.py:334
  440.4 159.2 %all-gather.8.cloned.1.call-start = ((), (), s32[]{:S(2)}) async-start(), calls=%async_computation.7 | async-start | bytes 6291456 | tf_op jit(solution)/shard_map/all_gather | solution.py:336
  542.0 8.3 %copy-start.6 = (f32[1,512,1024]{2,1,0:T(8,128)S(1)}, f32[1,512,1024]{2,1,0:T(8,128)}, u32[]{:S(2)}) copy-start(f32[1,512,1024]{2,1,0:T(8,128)} %copy-done.5) | copy-start | bytes 6291460
  542.0 8.3 %copy-start.45 = (bf16[1,16,1024]{2,0,1:T(2,128)(2,1)S(1)}, bf16[1,16,1024]{2,0,1:T(2,128)(2,1)}, u32[]{:S(2)}) copy-start(bf16[1,16,1024]{2,0,1:T(2,128)(2,1)} %copy-done.44) | copy-start | bytes 98308
  542.1 8.3 %copy-start.73 = (f32[1024]{0:T(1024)S(1)}, f32[1024]{0:T(1024)}, u32[]{:S(2)}) copy-start(f32[1024]{0:T(1024)} %param.46) | copy-start | bytes 12292
  553.0 6.8 %copy-start.56 = (bf16[1,16,1024]{2,0,1:T(2,128)(2,1)S(1)}, bf16[1,16,1024]{2,0,1:T(2,128)(2,1)}, u32[]{:S(2)}) copy-start(bf16[1,16,1024]{2,0,1:T(2,128)(2,1)} %copy-done.55) | copy-start | bytes 98308
  559.8 3.8 copy-start.9
  602.6 3.8 copy-start.1
  (30 other events, 59.8 us)
Sparse Core Ops, SparseCore 0:
  25.5 35.8 all-gather.5
  63.5 33.1 all-gather.3
  308.4 31.8 reduce-scatter.3
  342.4 31.8 reduce-scatter.5
  386.0 54.2 reduce-scatter.7
  444.2 97.8 all-reduce.1
  543.6 55.9 all-gather.7
where the time goes:
time: 622 us; the launch traced here: 614 us
  waiting for transfers between devices  274 us (44%)
  matrix products  227 us (36%)
  other arithmetic  47.6 us (8%)
  local copies, waits for them, and re-layouts  46.8 us (8%)
  between operations  16.4 us (3%)
    psum x1, waiting for transfers between devices, body(): summed = lax.psum(packed.astype(jnp.bfloat16), 'dp')  101 us
    reduce_scatter x1, waiting for transfers between devices, body(): lax.psum_scatter(summed, 'seq', scatter_dimension=2, tiled=True)  54.4 us
    all_gather x1, waiting for transfers between devices, body(): lax.all_gather(owned.astype(jnp.bfloat16), 'seq', axis=2, tiled=True)  32.4 us
    reduce_scatter x1, waiting for transfers between devices, body(): lax.psum_scatter(value_full.astype(jnp.bfloat16), 'seq', scatter_dimensio...  31.6 us
    reduce_scatter x1, waiting for transfers between devices, body(): lax.psum_scatter(key_full.astype(jnp.bfloat16), 'seq', scatter_dimension=...  27.5 us
    all_gather x1, waiting for transfers between devices, body(): lax.all_gather(key_low, 'seq', axis=1, tiled=True)  26.5 us
    dot_general x4, matrix products, project(): jnp.einsum('cra,cae->cre', low_rank, up_pick, preferred_element_type=jnp....  24.4 us
    dot_general x4, matrix products, project_back(): jnp.einsum('cre,de->crd', grad_low, weight, preferred_element_type=jnp.fl...  23 us
  transfers between devices with their start and end apart: 7, of which 6 were waited for; matrix products, arithmetic and copies ran while one was open for 12% of the time, Pallas kernels for 0%

commit v1 on v0

--- a/solution.py
+++ b/solution.py
@@ -331,7 +331,7 @@
     packed = jnp.einsum(
         "ca,crw->arw", onehot.astype(jnp.float32), packed_clip, precision=lax.Precision.HIGHEST
     )
-    summed = lax.psum(packed.astype(jnp.bfloat16), "dp")
+    summed = jnp.sum(lax.all_gather(packed.astype(jnp.bfloat16), "dp"), axis=0)
     owned = lax.psum_scatter(summed, "seq", scatter_dimension=2, tiled=True).astype(jnp.float32)
     gathered = lax.all_gather(owned.astype(jnp.bfloat16), "seq", axis=2, tiled=True).astype(
         owned.dtype

time: 622 us -> 858 us (1.38)
  waiting for transfers between devices: 274 us -> 500 us
  other arithmetic: 47.6 us -> 71.1 us
  matrix products: 227 us -> 209 us
    all_gather x0 -> x1, waiting for transfers between devices: none -> 326 us  [body(): summed = jnp.sum(lax.all_gather(packed.astype(jnp.bfloat16), 'dp'), axis=0)]
    psum x1 -> x0, waiting for transfers between devices: 101 us -> none  [body(): summed = lax.psum(packed.astype(jnp.bfloat16), 'dp')]
    reduce_sum x0 -> x1, other arithmetic: none -> 23.7 us  [body(): summed = jnp.sum(lax.all_gather(packed.astype(jnp.bfloat16), 'dp'), axis=0)]
    dot_general x2, matrix products: 12.9 us -> 3 us  [backward_step(): jnp.einsum('chqk,ckhd->cqhd', grad_score, key_heads, preferred_element_ty...]
  transfers between devices with their start and end apart: 7 -> 7, of which waited for: 6 -> 6; matrix products, arithmetic and copies ran while one was open for 12% -> 9% of each run, Pallas kernels for 0% -> 0%
where the time goes in v1:
time: 858 us; the launch traced here: 849 us
  waiting for transfers between devices  500 us (58%)
  matrix products  209 us (24%)
  other arithmetic  71.1 us (8%)
  local copies, waits for them, and re-layouts  51 us (6%)
  between operations  16.5 us (2%)
    all_gather x1, waiting for transfers between devices, body(): summed = jnp.sum(lax.all_gather(packed.astype(jnp.bfloat16), 'dp'), axis=0)  326 us
    reduce_scatter x1, waiting for transfers between devices, body(): lax.psum_scatter(summed, 'seq', scatter_dimension=2, tiled=True)  54.1 us
    all_gather x1, waiting for transfers between devices, body(): lax.all_gather(owned.astype(jnp.bfloat16), 'seq', axis=2, tiled=True)  33.2 us
    reduce_scatter x1, waiting for transfers between devices, body(): lax.psum_scatter(value_full.astype(jnp.bfloat16), 'seq', scatter_dimensio...  31.6 us
    reduce_scatter x1, waiting for transfers between devices, body(): lax.psum_scatter(key_full.astype(jnp.bfloat16), 'seq', scatter_dimension=...  27.5 us
    all_gather x1, waiting for transfers between devices, body(): lax.all_gather(key_low, 'seq', axis=1, tiled=True)  26.4 us
    dot_general x4, matrix products, project(): jnp.einsum('cra,cae->cre', low_rank, up_pick, preferred_element_type=jnp....  24.5 us
    reduce_sum x1, other arithmetic, body(): summed = jnp.sum(lax.all_gather(packed.astype(jnp.bfloat16), 'dp'), axis=0)  23.7 us
  transfers between devices with their start and end apart: 7, of which 6 were waited for; matrix products, arithmetic and copies ran while one was open for 9% of the time, Pallas kernels for 0%

profile of v1, /device:TPU:0, one launch (start us, length us, event | category | flops | bytes accessed | tf_op | source)
XLA Modules:
  0.0 848.8 jit_solution(4285656545800320498)
XLA Ops:
  9.6 1.6 fusion.44
  13.1 1.8 convolution_convert_fusion.5
  14.9 5.8 fusion.113
  22.5 2.6 copy-done.14
  26.3 4.8 fusion.116
  31.2 2.9 copy.50
  34.1 3.0 copy.49
  37.5 4.2 subtract_convert_fusion.2
  43.7 1.8 fusion.75
  47.8 1.8 fusion.73
  51.0 2.5 fusion.66
  53.6 3.2 fusion.64
  56.8 10.4 %fusion.62 = f32[512,4096]{1,0:T(8,128)} fusion(bf16[4096,1024]{1,0:T(8,128)(2,1)} %param.45, bf16[1,512,1024]{2,1,0:T(8,128)(2,1)S(1)} %copy-done.24), kind=kOutput, calls=%fused_computation.125 | convolution fusion | flops 4294967296 | bytes 17825792 | tf_op jit(solution)/shard_map/cre,de->crd/dot_general | solution.py:99
  67.1 3.9 copy.51
  71.1 26.4 %all-gather.6.cloned.1.call-done = bf16[1,1024,1024]{1,2,0:T(8,128)(2,1)} async-done(((bf16[1,512,1024]{1,2,0:T(8,128)(2,1)}), bf16[1,1024,1024]{1,2,0:T(8,128)(2,1)}) %all-gather.6.cloned.1.call-update) | async-done | bytes 2097168 | tf_op jit(solution)/shard_map/all_gather | solution.py:214
  97.5 58.6 %while.36 = (s32[]{:T(128)}, f32[1,16,512]{2,1,0:T(8,128)S(1)}, f32[1,16,512]{2,1,0:T(8,128)S(1)}, f32[1,512,16,64]{1,3,2,0:T(8,128)}, bf16[1,1024,1024]{1,2,0:T...) while((s32[]{:T(128)}, f32[1,16,512]{2,1,0:T(8,128)S(1)}, ...), condition=%wide.region_5.6_spmd.clone, body=%wide.region_2.5_spmd.clone.sunk | while | flops 1108918272 | bytes 62390448 | solution.py:125
  97.5 1.7 constant_dynamic-slice_fusion.7
  99.2 8.2 bitcast_reduce_fusion.2
  107.4 8.6 %fusion.188 = f32[16,512]{1,0:T(8,128)S(1)} fusion(f32[16,512,512]{2,1,0:T(8,128)} %get-tuple-element.604, f32[16,512]{1,0:T(8,128)S(1)} %bitcast.343), kind=kLoop, calls=%fused_computation.4.clone.1 | loop fusion | flops 12574720 | bytes 16842752 | tf_op jit(solution)/shard_map/while/body/eval_jaxpr/reduce_sum | solution.py:198
  116.0 10.3 %bitcast_add_fusion.8 = f32[1,512,16,64]{1,3,2,0:T(8,128)} fusion(f32[1,512,16,64]{1,3,2,0:T(8,128)} %get-tuple-element.633, bf16[512,16,64]{0,2,1:T(8,128)(2,1)S(1)} %bitcast.338, f32[16,512,512]{2,1,0:T(8,128)} %get-tuple-element.604, f32[16,512]{1,0:T(8,128)S(1)} %bitcast.344, f32[512,16]{0,1:T(8,128)S(1)} %get-tuple-element.606, pred[]{:T(512)S(6)} %compare.27), kind=kOutput, calls=%fused_computation.8.clone.1 | convolution fusion | flops 551026688 | bytes 22085632 | tf_op jit(solution)/shard_map/while/body/eval_jaxpr/chqk,ckhd->cqhd/dot_general | solution.py:199
  126.3 1.7 constant_dynamic-slice_fusion.7
  128.0 8.2 bitcast_reduce_fusion.2
  136.2 8.6 %fusion.188 = f32[16,512]{1,0:T(8,128)S(1)} fusion(f32[16,512,512]{2,1,0:T(8,128)} %get-tuple-element.604, f32[16,512]{1,0:T(8,128)S(1)} %bitcast.343), kind=kLoop, calls=%fused_computation.4.clone.1 | loop fusion | flops 12574720 | bytes 16842752 | tf_op jit(solution)/shard_map/while/body/eval_jaxpr/reduce_sum | solution.py:198
  144.8 10.9 %bitcast_add_fusion.8 = f32[1,512,16,64]{1,3,2,0:T(8,128)} fusion(f32[1,512,16,64]{1,3,2,0:T(8,128)} %get-tuple-element.633, bf16[512,16,64]{0,2,1:T(8,128)(2,1)S(1)} %bitcast.338, f32[16,512,512]{2,1,0:T(8,128)} %get-tuple-element.604, f32[16,512]{1,0:T(8,128)S(1)} %bitcast.344, f32[512,16]{0,1:T(8,128)S(1)} %get-tuple-element.606, pred[]{:T(512)S(6)} %compare.27), kind=kOutput, calls=%fused_computation.8.clone.1 | convolution fusion | flops 551026688 | bytes 22085632 | tf_op jit(solution)/shard_map/while/body/eval_jaxpr/chqk,ckhd->cqhd/dot_general | solution.py:199
  156.1 2.0 fusion.68
  162.5 1.7 slice-done.1
  164.2 4.5 fusion.121
  168.8 21.4 %multiply_convert_fusion.2 = (bf16[512,4096]{1,0:T(8,128)(2,1)}, f32[512,4096]{1,0:T(8,128)}, f32[512,4096]{1,0:T(8,128)}) fusion(bf16[512,16]{0,1:T(8,128)(2,1)S(1)} %convolution_convert_fusion.4, bf16[1,16,4096]{2,0,1:T(2,128)(2,1)S(1)} %fusion.66, f32[512,4096]{1,0:T(8,128)S(1)} %fusion.121, f32[4096]{0:T(1024)S(1)} %copy-done.75), kind=kOutput, calls=%fused_computation.42 | convolution fusion | flops 207618048 | bytes 29523968 | tf_op jit(solution)/shard_map/cra,cae->cre/dot_general | solution.py:94
  190.2 10.5 %add_convert_fusion = bf16[512,4096]{1,0:T(8,128)(2,1)S(1)} fusion(f32[512,4096]{1,0:T(8,128)} %get-tuple-element.458, f32[512,4096]{1,0:T(8,128)} %fusion.62, f32[512,4096]{1,0:T(8,128)} %get-tuple-element.490, bf16[16,512]{1,0:T(8,128)(2,1)S(1)} %copy-done.56, bf16[1,16,4096]{2,0,1:T(2,128)(2,1)S(1)} %copy-done.37), kind=kOutput, calls=%fused_computation.41 | convolution fusion | flops 98566144 | bytes 29507584 | tf_op jit(solution)/shard_map/cra,cad->crd/dot_general | solution.py:103
  201.9 4.5 fusion.123
  206.5 2.0 fusion.45
  208.5 1.8 reduce_sum.112
  210.3 3.2 fusion.47
  216.3 2.0 multiply_reduce_fusion
  218.3 1.6 broadcast.568.clone
  221.6 71.3 %while.37 = (s32[]{:T(128)}, f32[1,512,16,64]{1,3,2,0:T(8,128)}, bf16[1,1024,1024]{1,2,0:T(8,128)(2,1)}, bf16[1,1024,1024]{1,2,0:T(8,128)(2,1)}, bf16[1,1024,102...) while((s32[]{:T(128)}, f32[1,512,16,64]{1,3,2,0:T(8,128)}, ...), condition=%wide.region_12.13_spmd.clone, body=%wide.region_11.12_spmd.clone.sunk | while | flops 2720530432 | bytes 135364960 | solution.py:125
  221.8 2.3 constant_dynamic-slice_fusion.9
  225.3 8.2 fusion.199
  233.5 8.5 %fusion.200 = bf16[16,512,64]{1,2,0:T(8,128)(2,1)} fusion(f32[16,512,512]{2,1,0:T(8,128)} %fusion.199, f32[16,512]{1,0:T(8,128)S(1)} %bitcast.351, bf16[1,512,16,64]{1,3,2,0:T(8,128)(2,1)S(1)} %get-tuple-element.688), kind=kOutput, calls=%fused_computation.23.clone.1 | convolution fusion | flops 549453824 | bytes 18907136 | tf_op jit(solution)/shard_map/while/body/eval_jaxpr/chqk,cqhd->ckhd/dot_general | solution.py:284
  242.0 8.5 %multiply_convert_fusion.4 = bf16[16,512,512]{2,1,0:T(8,128)(2,1)S(1)} fusion(f32[16,512,512]{2,1,0:T(8,128)} %fusion.199, bf16[512,16,64]{0,2,1:T(8,128)(2,1)} %bitcast.341, f32[16,512]{1,0:T(8,128)S(1)} %bitcast.356, f32[16,512]{1,0:T(8,128)S(1)} %bitcast.352, bf16[1,512,16,64]{1,3,2,0:T(8,128)(2,1)S(1)} %get-tuple-element.688), kind=kOutput, calls=%fused_computation.20.clone.1 | convolution fusion | flops 557842432 | bytes 27328512 | tf_op jit(solution)/shard_map/while/body/eval_jaxpr/cqhd,ckhd->chqk/dot_general | solution.py:258
  252.1 2.6 convolution_multiply_fusion.2
  257.3 2.3 constant_dynamic-slice_fusion.9
  260.9 8.2 fusion.199
  269.0 8.5 %fusion.200 = bf16[16,512,64]{1,2,0:T(8,128)(2,1)} fusion(f32[16,512,512]{2,1,0:T(8,128)} %fusion.199, f32[16,512]{1,0:T(8,128)S(1)} %bitcast.351, bf16[1,512,16,64]{1,3,2,0:T(8,128)(2,1)S(1)} %get-tuple-element.688), kind=kOutput, calls=%fused_computation.23.clone.1 | convolution fusion | flops 549453824 | bytes 18907136 | tf_op jit(solution)/shard_map/while/body/eval_jaxpr/chqk,cqhd->ckhd/dot_general | solution.py:284
  277.5 8.5 %multiply_convert_fusion.4 = bf16[16,512,512]{2,1,0:T(8,128)(2,1)S(1)} fusion(f32[16,512,512]{2,1,0:T(8,128)} %fusion.199, bf16[512,16,64]{0,2,1:T(8,128)(2,1)} %bitcast.341, f32[16,512]{1,0:T(8,128)S(1)} %bitcast.356, f32[16,512]{1,0:T(8,128)S(1)} %bitcast.352, bf16[1,512,16,64]{1,3,2,0:T(8,128)(2,1)S(1)} %get-tuple-element.688), kind=kOutput, calls=%fused_computation.20.clone.1 | convolution fusion | flops 557842432 | bytes 27328512 | tf_op jit(solution)/shard_map/while/body/eval_jaxpr/cqhd,ckhd->chqk/dot_general | solution.py:258
  287.6 2.6 convolution_multiply_fusion.2
  293.8 3.5 convolution_convert_fusion.7
  297.4 27.5 %reduce-scatter.4.cloned.1.call-done = bf16[1,512,1024]{1,2,0:T(8,128)(2,1)} async-done(((bf16[1,1024,1024]{1,2,0:T(8,128)(2,1)}), bf16[1,512,1024]{1,2,0:T(8,128)(2,1)}) %reduce-scatter.4.cloned.1.call-update) | async-done | bytes 1048592 | tf_op jit(solution)/shard_map/reduce_scatter | solution.py:307
  327.3 31.6 %reduce-scatter.6.cloned.1.call-done = bf16[1,512,1024]{1,2,0:T(8,128)(2,1)} async-done(((bf16[1,1024,1024]{1,2,0:T(8,128)(2,1)}), bf16[1,512,1024]{1,2,0:T(8,128)(2,1)}) %reduce-scatter.6.cloned.1.call-update) | async-done | bytes 1048592 | tf_op jit(solution)/shard_map/reduce_scatter | solution.py:310
  358.9 1.8 convolution_convert_fusion
  361.5 2.6 fusion.32
  367.9 2.7 multiply_convert_fusion.1
  370.6 326.2 %all-gather.12.cloned.1.call-done = bf16[128,16,16384]{2,1,0:T(8,128)(2,1)} async-done(((bf16[8,16,16384]{2,1,0:T(8,128)(2,1)}), bf16[128,16,16384]{2,1,0:T(8,128)(2,1)}) %all-gather.12.cloned.1.call-update) | async-done | bytes 67108880 | tf_op jit(solution)/shard_map/all_gather | solution.py:334
  696.8 23.7 %reduce_sum.118 = bf16[8,16,16384]{2,1,0:T(8,128)(2,1)} reduce(bf16[16,8,16,16384]{3,2,1,0:T(8,128)(2,1)} %bitcast.52, bf16[]{:T(256)} %constant.235.clone.1), dimensions={0}, to_apply=%region_17.18 | reduce | flops 31457280 | bytes 71303168 | tf_op jit(solution)/shard_map/reduce_sum | solution.py:334
  720.9 54.1 %reduce-scatter.8.cloned.1.call-done = bf16[8,16,8192]{2,1,0:T(8,128)(2,1)} async-done(((bf16[8,16,16384]{2,1,0:T(8,128)(2,1)}), bf16[8,16,8192]{2,1,0:T(8,128)(2,1)}) %reduce-scatter.8.cloned.1.call-update) | async-done | bytes 2097168 | tf_op jit(solution)/shard_map/reduce_scatter | solution.py:335
  775.0 8.3 fusion.122
  786.1 6.8 fusion.110
  792.9 2.0 fusion.40
  794.9 1.8 reduce_sum.116
  796.7 3.5 fusion.43
  800.2 33.2 %all-gather.10.cloned.1.call-done = bf16[8,16,16384]{2,1,0:T(8,128)(2,1)} async-done(((bf16[8,16,8192]{2,1,0:T(8,128)(2,1)}), bf16[8,16,16384]{2,1,0:T(8,128)(2,1)}) %all-gather.10.cloned.1.call-update) | async-done | bytes 4194320 | tf_op jit(solution)/shard_map/all_gather | solution.py:336
  833.4 2.6 slice.87
  836.0 3.0 fusion.117
  838.9 2.5 fusion.118
  (249 shorter events, 43.7 us)
Async XLA Ops:
  7.2 152.1 %copy-start = (bf16[1024,1024]{1,0:T(8,128)(2,1)S(1)}, bf16[1024,1024]{1,0:T(8,128)(2,1)}, u32[]{:S(2)}) copy-start(bf16[1024,1024]{1,0:T(8,128)(2,1)} %param.35) | copy-start | bytes 6291460
  7.2 7.7 copy-start.11
  7.2 7.7 copy-start.69
  7.2 7.7 copy-start.76
  7.2 59.9 %all-gather.8.cloned.1.call-start = ((), (), s32[]{:S(2)}) async-start(), calls=%async_computation.4 | async-start | bytes 3145728 | tf_op jit(solution)/shard_map/all_gather | solution.py:215
  9.6 11.2 %copy-start.60 = (f32[512]{0:T(512)}, f32[512]{0:T(512)S(1)}, u32[]{:S(2)}) copy-start(f32[512]{0:T(512)S(1)} %broadcast_multiply_fusion.5) | copy-start | bytes 6148
  11.2 9.6 %copy-start.62 = (f32[512]{0:T(512)}, f32[512]{0:T(512)S(1)}, u32[]{:S(2)}) copy-start(f32[512]{0:T(512)S(1)} %add_rsqrt_fusion.1) | copy-start | bytes 6148
  14.9 6.6 copy-start.64
  14.9 5.9 copy-start.32
  14.9 6.5 copy-start.67
  26.3 71.2 %all-gather.6.cloned.1.call-start = ((), (), s32[]{:S(2)}) async-start(), calls=%async_computation.3 | async-start | bytes 3145728 | tf_op jit(solution)/shard_map/all_gather | solution.py:214
  37.5 5.3 copy-start.33
  37.5 5.3 copy-start.35
  37.5 5.3 copy-start.47
  37.5 9.3 %copy-start.23 = (bf16[1,512,1024]{2,1,0:T(8,128)(2,1)S(1)}, bf16[1,512,1024]{2,1,0:T(8,128)(2,1)}, u32[]{:S(2)}) copy-start(bf16[1,512,1024]{2,1,0:T(8,128)(2,1)} %param.49) | copy-start | bytes 3145732
  42.8 282.1 %reduce-scatter.4.cloned.1.call-start = ((), (), s32[]{:S(2)}) async-start(), calls=%async_computation.5 | async-start | bytes 3145728 | tf_op jit(solution)/shard_map/reduce_scatter | solution.py:307
  49.7 7.1 copy-start.24
  156.1 4.5 copy-start.12
  156.1 4.5 copy-start.41
  156.1 4.5 copy-start.71
  158.1 3.2 copy-start.15
  159.3 3.3 slice-start
  160.6 3.6 slice-start.1
  161.3 45.1 %copy-start.6 = (f32[1,512,1024]{2,1,0:T(8,128)}, f32[1,512,1024]{2,1,0:T(8,128)S(1)}, u32[]{:S(2)}) copy-start(f32[1,512,1024]{2,1,0:T(8,128)S(1)} %get-tuple-element.489) | copy-start | bytes 6291460
  162.2 6.6 copy-start.21
  164.2 4.5 copy-start.58
  164.2 4.5 copy-start.75
  168.8 21.4 %copy-start.37 = (bf16[1,16,4096]{2,0,1:T(2,128)(2,1)S(1)}, bf16[1,16,4096]{2,0,1:T(2,128)(2,1)}, u32[]{:S(2)}) copy-start(bf16[1,16,4096]{2,0,1:T(2,128)(2,1)} %fusion.64) | copy-start | bytes 393220
  168.8 21.4 %copy-start.56 = (bf16[16,512]{1,0:T(8,128)(2,1)S(1)}, bf16[16,512]{1,0:T(8,128)(2,1)}, u32[]{:S(2)}) copy-start(bf16[16,512]{1,0:T(8,128)(2,1)} %convolution_convert_fusion.3) | copy-start | bytes 49156
  200.7 5.8 copy-start.18
  201.9 4.6 copy-start.50
  210.3 3.3 copy-start.42
  242.0 8.5 %copy-start.2 = (f32[1,512,16,64]{1,3,2,0:T(8,128)S(1)}, f32[1,512,16,64]{1,3,2,0:T(8,128)}, u32[]{:S(2)}) copy-start(f32[1,512,16,64]{1,3,2,0:T(8,128)} %get-tuple-element.667) | copy-start | bytes 6291460 | tf_op jit(solution)/shard_map/while
  277.5 8.5 %copy-start.2 = (f32[1,512,16,64]{1,3,2,0:T(8,128)S(1)}, f32[1,512,16,64]{1,3,2,0:T(8,128)}, u32[]{:S(2)}) copy-start(f32[1,512,16,64]{1,3,2,0:T(8,128)} %get-tuple-element.667) | copy-start | bytes 6291460 | tf_op jit(solution)/shard_map/while
  292.9 66.0 %reduce-scatter.6.cloned.1.call-start = ((), (), s32[]{:S(2)}) async-start(), calls=%async_computation.6 | async-start | bytes 3145728 | tf_op jit(solution)/shard_map/reduce_scatter | solution.py:310
  293.5 32.9 %copy-start.4 = (f32[1,512,16,64]{1,3,2,0:T(8,128)S(1)}, f32[1,512,16,64]{1,3,2,0:T(8,128)}, u32[]{:S(2)}) copy-start(f32[1,512,16,64]{1,3,2,0:T(8,128)} %get-tuple-element.310) | copy-start | bytes 6291460
  293.5 32.9 %copy-start.34 = (f32[512,32]{0,1:T(8,128)S(1)}, f32[512,32]{0,1:T(8,128)}, u32[]{:S(2)}) copy-start(f32[512,32]{0,1:T(8,128)} %copy-done.33) | copy-start | bytes 196612
  293.5 32.9 %copy-start.36 = (f32[512,32]{0,1:T(8,128)S(1)}, f32[512,32]{0,1:T(8,128)}, u32[]{:S(2)}) copy-start(f32[512,32]{0,1:T(8,128)} %copy-done.35) | copy-start | bytes 196612
  293.5 403.3 %all-gather.12.cloned.1.call-start = ((), (), s32[]{:S(2)}) async-start(), calls=%async_computation.9 | async-start | bytes 71303168 | tf_op jit(solution)/shard_map/all_gather | solution.py:334
  326.4 32.5 %copy-start.40 = (bf16[1,16,3072]{2,0,1:T(2,128)(2,1)S(1)}, bf16[1,16,3072]{2,0,1:T(2,128)(2,1)}, u32[]{:S(2)}) copy-start(bf16[1,16,3072]{2,0,1:T(2,128)(2,1)} %copy-done.39) | copy-start | bytes 294916
  327.2 33.6 %copy-start.28 = (bf16[1,512,16,64]{1,3,2,0:T(8,128)(2,1)}, bf16[1,512,16,64]{1,3,2,0:T(8,128)(2,1)S(1)}, u32[]{:S(2)}) copy-start(bf16[1,512,16,64]{1,3,2,0:T(8,128)(2,1)S(1)} %pad_maximum_fusion.3) | copy-start | bytes 3145732
  327.2 33.5 %copy-start.30 = (bf16[1,512,16,64]{1,3,2,0:T(8,128)(2,1)}, bf16[1,512,16,64]{1,3,2,0:T(8,128)(2,1)S(1)}, u32[]{:S(2)}) copy-start(bf16[1,512,16,64]{1,3,2,0:T(8,128)(2,1)S(1)} %pad_maximum_fusion.4) | copy-start | bytes 3145732
  327.3 33.5 %copy-start.13 = (bf16[1,512,1024]{2,1,0:T(8,128)(2,1)S(1)}, bf16[1,512,1024]{2,1,0:T(8,128)(2,1)}, u32[]{:S(2)}) copy-start(bf16[1,512,1024]{2,1,0:T(8,128)(2,1)} %param.27) | copy-start | bytes 3145732
  327.3 33.5 %copy-start.61 = (f32[512]{0:T(512)S(1)}, f32[512]{0:T(512)}, u32[]{:S(2)}) copy-start(f32[512]{0:T(512)} %copy-done.60) | copy-start | bytes 6148
  327.3 33.5 %copy-start.63 = (f32[512]{0:T(512)S(1)}, f32[512]{0:T(512)}, u32[]{:S(2)}) copy-start(f32[512]{0:T(512)} %copy-done.62) | copy-start | bytes 6148
  327.3 33.5 %copy-start.70 = (f32[1024]{0:T(1024)S(1)}, f32[1024]{0:T(1024)}, u32[]{:S(2)}) copy-start(f32[1024]{0:T(1024)} %param.29) | copy-start | bytes 12292
  327.3 33.5 %copy-start.77 = (f32[1024]{0:T(1024)S(1)}, f32[1024]{0:T(1024)}, u32[]{:S(2)}) copy-start(f32[1024]{0:T(1024)} %param.30) | copy-start | bytes 12292
  360.8 3.3 copy-start.53
  361.4 3.1 copy-start.9
  361.4 3.1 copy-start.49
  361.4 3.3 copy-start.22
  361.4 3.3 copy-start.51
  361.4 4.1 copy-start.19
  361.5 4.1 copy-start.59
  364.1 2.8 copy-start.17
  370.6 404.4 %reduce-scatter.8.cloned.1.call-start = ((), (), s32[]{:S(2)}) async-start(), calls=%async_computation.7 | async-start | bytes 6291456 | tf_op jit(solution)/shard_map/reduce_scatter | solution.py:335
  720.5 112.8 %all-gather.10.cloned.1.call-start = ((), (), s32[]{:S(2)}) async-start(), calls=%async_computation.8 | async-start | bytes 6291456 | tf_op jit(solution)/shard_map/all_gather | solution.py:336
  775.0 8.3 copy-start.7
  775.0 8.3 copy-start.44
  775.0 8.3 copy-start.72
  786.1 6.8 copy-start.55
  792.9 3.8 copy-start.10
  833.4 5.5 copy-start.20
  836.0 5.4 copy-start.1
  (28 other events, 54.5 us)
Sparse Core Ops, SparseCore 0:
  26.4 35.7 all-gather.7
  64.4 33.1 all-gather.5
  293.0 31.8 reduce-scatter.3
  327.0 31.8 reduce-scatter.5
  370.7 326.1 all-gather.11
  720.7 54.2 reduce-scatter.7
  776.6 56.7 all-gather.9
